TPU v7x, 32 devices: a whole 2x2x4 slice. The times are simulated.
32 devices in a mesh: dp: 16 (over z, y, x), tensor: 2 (over core).
Axes of the slice: x: 2, y: 2, z: 4, core: 2. Of those that a mesh axis runs over, the one named last changes fastest.
Arguments:
- tokens: bfloat16 [4096, 768], P(('dp', 'tensor')), may hold values from -6 to 6
- segments: int32 [4096], P('dp'), may hold values from 0 to 7, as said below
- attention_gain: float32 [768], replicated, may hold values from 0.1 to 1.9
- attention_shift: float32 [768], replicated, may hold values from -3 to 3
- query_key_value: bfloat16 [768, 3, 768], P(None, None, 'tensor'), may hold values from -0.21875 to 0.21875
- query_value_bias: float32 [2, 768], P(None, 'tensor'), may hold values from -3 to 3
- output_weight: bfloat16 [768, 768], P('tensor'), may hold values from -0.875 to 0.875
- output_bias: float32 [768], replicated, may hold values from -3 to 3
- feedforward_gain: float32 [768], replicated, may hold values from 0.1 to 1.9
- feedforward_shift: float32 [768], replicated, may hold values from -3 to 3
- expand_weight: bfloat16 [768, 3072], P(None, 'tensor'), may hold values from -0.21875 to 0.21875
- expand_bias: float32 [3072], P('tensor'), may hold values from -3 to 3
- contract_weight: bfloat16 [3072, 768], P('tensor'), may hold values from -0.21875 to 0.21875
- contract_bias: float32 [768], replicated, may hold values from -3 to 3
- cotangent: bfloat16 [4096, 768], P(('dp', 'tensor')), may hold values from -6 to 6
Outputs:
- block_output: float32 [4096, 768], P(('dp', 'tensor'))
- input_gradient: float32 [4096, 768], P(('dp', 'tensor'))
- attention_gain_gradient: float32 [768], replicated
- attention_shift_gradient: float32 [768], replicated
- query_key_value_gradient: float32 [768, 3, 768], P('dp', None, 'tensor')
- query_value_bias_gradient: float32 [2, 768], P(None, 'tensor')
- output_weight_gradient: float32 [768, 768], P('tensor', 'dp')
- output_bias_gradient: float32 [768], replicated
- feedforward_gain_gradient: float32 [768], replicated
- feedforward_shift_gradient: float32 [768], replicated
- expand_weight_gradient: float32 [768, 3072], P('dp', 'tensor')
- expand_bias_gradient: float32 [3072], P('tensor')
- contract_weight_gradient: float32 [3072, 768], P('tensor', 'dp')
- contract_bias_gradient: float32 [768], replicated
Inputs may be any that keep to these rules, and one draw needn't show every extreme that they name: `segments`: within each pack of 256 tokens the numbers start at 0, never fall and rise by at most one from token to token; a sequence is a run of one number in one pack and holds 1 to 256 tokens; some sequence holds exactly 256; some pack holds 8 sequences.
All inputs are finite; a program needn't handle non-finite values.
Results may differ from a plain program's by a relative error of at most 0.012.
The roundings to bfloat16 on the way count: a program that leaves them out, or rounds other values in their place, can miss the bound.
Values may be sent and summed in bfloat16 or wider, within the bound.
A program may use at most 128 MiB of HBM per device.

v0:
```python
import jax
import jax.numpy as jnp
from jax import lax
from jax.sharding import PartitionSpec as P

HEAD_DIM = 64
epsilon = 1e-05


def normalize(values, gain, shift):
    center = jnp.mean(values, axis=-1, keepdims=True)
    centered = values - center
    spread = jnp.mean(centered * centered, axis=-1, keepdims=True)
    inverse = lax.rsqrt(spread + epsilon)
    unit = centered * inverse
    return (unit * gain + shift, unit, inverse)


def normalize_back(unit, inverse, gain, incoming):
    scaled = incoming * gain
    first = jnp.mean(scaled, axis=-1, keepdims=True)
    second = jnp.mean(scaled * unit, axis=-1, keepdims=True)
    return inverse * (scaled - first - unit * second)


def gelu_tanh(values):
    return jax.nn.gelu(values, approximate=True)


def allowed_pairs(segments):
    count = segments.shape[0]
    query_place = lax.broadcasted_iota(jnp.int32, (count, count), 0)
    key_place = lax.broadcasted_iota(jnp.int32, (count, count), 1)
    return (key_place <= query_place) & (segments[:, None] == segments[None, :])


def contract_rows(left, right):
    return lax.dot_general(
        left, right, (((0,), (0,)), ((), ())), preferred_element_type=jnp.float32
    )


def contract_columns(left, right):
    return lax.dot_general(
        left, right, (((1,), (1,)), ((), ())), preferred_element_type=jnp.float32
    )


def attention_weights(query, keys, allowed, scale, log_total):
    scores = jnp.einsum("qhe,khe->hqk", query, keys, preferred_element_type=jnp.float32) * scale
    masked = jnp.where(allowed, scores, -1e30)
    return jnp.where(allowed, jnp.exp(masked - log_total), 0.0)


def shards(
    tokens,
    segments,
    attention_gain,
    attention_shift,
    query_key_value,
    query_value_bias,
    output_weight,
    output_bias,
    feedforward_gain,
    feedforward_shift,
    expand_weight,
    expand_bias,
    contract_weight,
    contract_bias,
    cotangent,
):
    width = tokens.shape[1]
    local = query_key_value.shape[2]
    heads_here = local // HEAD_DIM
    scale = HEAD_DIM ** (-0.5)
    flat_weight = query_key_value.reshape(width, 3 * local)
    residual_in = tokens.astype(jnp.float32)
    normed_share, unit_one, inverse_one = normalize(residual_in, attention_gain, attention_shift)
    normed_share = normed_share.astype(jnp.bfloat16)
    normed_one, cotangent_rows = (
        lax.all_gather(normed_share, "tensor", axis=0, tiled=True),
        lax.all_gather(cotangent, "tensor", axis=0, tiled=True),
    )
    length = normed_one.shape[0]
    joined = jnp.dot(normed_one, flat_weight, preferred_element_type=jnp.float32).reshape(
        length, 3, local
    )
    query = (
        (joined[:, 0] + query_value_bias[0])
        .astype(jnp.bfloat16)
        .reshape(length, heads_here, HEAD_DIM)
    )
    keys = joined[:, 1].astype(jnp.bfloat16).reshape(length, heads_here, HEAD_DIM)
    values = (
        (joined[:, 2] + query_value_bias[1])
        .astype(jnp.bfloat16)
        .reshape(length, heads_here, HEAD_DIM)
    )
    allowed = allowed_pairs(segments)[None]
    scores = jnp.einsum("qhe,khe->hqk", query, keys, preferred_element_type=jnp.float32) * scale
    masked = jnp.where(allowed, scores, -1e30)
    highest = jnp.max(masked, axis=2, keepdims=True)
    log_total = highest + jnp.log(jnp.sum(jnp.exp(masked - highest), axis=2, keepdims=True))
    weights_low = jnp.where(allowed, jnp.exp(masked - log_total), 0.0).astype(jnp.bfloat16)
    mixed = jnp.einsum("hqk,khe->qhe", weights_low, values, preferred_element_type=jnp.float32)
    mixed = mixed.astype(jnp.bfloat16)
    mixed_flat = mixed.reshape(length, local)
    partial_attention = jnp.dot(mixed_flat, output_weight, preferred_element_type=jnp.float32)
    attention_share = lax.psum_scatter(partial_attention, "tensor", scatter_dimension=0, tiled=True)
    hidden = residual_in + attention_share + output_bias
    normed_two_share, unit_two, inverse_two = normalize(hidden, feedforward_gain, feedforward_shift)
    normed_two = lax.all_gather(normed_two_share.astype(jnp.bfloat16), "tensor", axis=0, tiled=True)
    before = jnp.dot(normed_two, expand_weight, preferred_element_type=jnp.float32) + expand_bias
    after, gelu_back = jax.vjp(gelu_tanh, before)
    after_low = after.astype(jnp.bfloat16)
    partial_feed = jnp.dot(after_low, contract_weight, preferred_element_type=jnp.float32)
    block_output = (
        hidden
        + lax.psum_scatter(partial_feed, "tensor", scatter_dimension=0, tiled=True)
        + contract_bias
    )
    upstream = cotangent.astype(jnp.float32)
    contract_bias_grad = jnp.sum(upstream, axis=0)
    contract_grad = contract_rows(after_low, cotangent_rows)
    d_after = contract_columns(cotangent_rows, contract_weight)
    d_before = gelu_back(d_after)[0]
    expand_bias_grad = jnp.sum(d_before, axis=0)
    d_before_low = d_before.astype(jnp.bfloat16)
    expand_grad = contract_rows(normed_two, d_before_low)
    partial_second = contract_columns(d_before_low, expand_weight)
    d_normed_two = lax.psum_scatter(partial_second, "tensor", scatter_dimension=0, tiled=True)
    feed_gain_grad = jnp.sum(d_normed_two * unit_two, axis=0)
    feed_shift_grad = jnp.sum(d_normed_two, axis=0)
    d_hidden = upstream + normalize_back(unit_two, inverse_two, feedforward_gain, d_normed_two)
    output_bias_grad = jnp.sum(d_hidden, axis=0)
    d_hidden_low = lax.all_gather(d_hidden.astype(jnp.bfloat16), "tensor", axis=0, tiled=True)
    output_grad = contract_rows(mixed_flat, d_hidden_low)
    d_mixed = contract_columns(d_hidden_low, output_weight).astype(jnp.bfloat16)
    d_mixed = d_mixed.reshape(length, heads_here, HEAD_DIM)
    weights = attention_weights(query, keys, allowed, scale, log_total)
    weights_again = weights.astype(jnp.bfloat16)
    d_weights = jnp.einsum("qhe,khe->hqk", d_mixed, values, preferred_element_type=jnp.float32)
    delta = jnp.einsum("qhe,qhe->hq", d_mixed, mixed, preferred_element_type=jnp.float32)
    d_scores = (weights * (d_weights - delta[:, :, None]) * scale).astype(jnp.bfloat16)
    d_values = jnp.einsum(
        "hqk,qhe->khe", weights_again, d_mixed, preferred_element_type=jnp.float32
    )
    d_query = jnp.einsum("hqk,khe->qhe", d_scores, keys, preferred_element_type=jnp.float32)
    d_keys = jnp.einsum("hqk,qhe->khe", d_scores, query, preferred_element_type=jnp.float32)
    d_query = d_query.reshape(length, local)
    d_keys = d_keys.reshape(length, local)
    d_values = d_values.reshape(length, local)
    bias_grad = jnp.stack([jnp.sum(d_query, axis=0), jnp.sum(d_values, axis=0)])
    d_joined_low = (
        jnp.stack([d_query, d_keys, d_values], axis=1)
        .astype(jnp.bfloat16)
        .reshape(length, 3 * local)
    )
    joined_grad = contract_rows(normed_one, d_joined_low).reshape(width, 3, local)
    partial_first = contract_columns(d_joined_low, flat_weight)
    d_normed_one = lax.psum_scatter(partial_first, "tensor", scatter_dimension=0, tiled=True)
    first_gain_grad = jnp.sum(d_normed_one * unit_one, axis=0)
    first_shift_grad = jnp.sum(d_normed_one, axis=0)
    input_gradient = d_hidden + normalize_back(unit_one, inverse_one, attention_gain, d_normed_one)
    joined_share, output_share, expand_share, contract_share = (
        lax.psum_scatter(joined_grad, "dp", scatter_dimension=0, tiled=True),
        lax.psum_scatter(output_grad, "dp", scatter_dimension=1, tiled=True),
        lax.psum_scatter(expand_grad, "dp", scatter_dimension=0, tiled=True),
        lax.psum_scatter(contract_grad, "dp", scatter_dimension=1, tiled=True),
    )
    row_sums = lax.psum(
        (
            first_gain_grad,
            first_shift_grad,
            output_bias_grad,
            feed_gain_grad,
            feed_shift_grad,
            contract_bias_grad,
        ),
        ("dp", "tensor"),
    )
    unit_sums = lax.psum((bias_grad, expand_bias_grad), "dp")
    return (
        block_output,
        input_gradient,
        row_sums[0],
        row_sums[1],
        joined_share,
        unit_sums[0],
        output_share,
        row_sums[2],
        row_sums[3],
        row_sums[4],
        expand_share,
        unit_sums[1],
        contract_share,
        row_sums[5],
    )


def solution(mesh):
    in_specs = (
        P(("dp", "tensor"), None),
        P("dp"),
        P(),
        P(),
        P(None, None, "tensor"),
        P(None, "tensor"),
        P("tensor", None),
        P(),
        P(),
        P(),
        P(None, "tensor"),
        P("tensor"),
        P("tensor", None),
        P(),
        P(("dp", "tensor"), None),
    )
    out_specs = (
        P(("dp", "tensor"), None),
        P(("dp", "tensor"), None),
        P(),
        P(),
        P("dp", None, "tensor"),
        P(None, "tensor"),
        P("tensor", "dp"),
        P(),
        P(),
        P(),
        P("dp", "tensor"),
        P("tensor"),
        P("tensor", "dp"),
        P(),
    )
    return jax.shard_map(shards, mesh=mesh, in_specs=in_specs, out_specs=out_specs, check_vma=False)
```

profile of v0, /device:TPU:0, one launch (start us, length us, event | category | flops | bytes accessed | tf_op | source)
XLA Modules:
  0.0 668.4 jit_solution(5672348374279710601)
XLA Ops:
  11.2 2.2 all_gather.12
  13.4 3.9 copy.44
  17.3 2.2 fusion
  28.0 2.1 all_gather.14
  30.9 3.7 fusion.50
  34.5 4.4 reduce-scatter.9.cloned.1.call-done
  41.2 2.1 all_gather.13
  43.4 3.5 fusion.42
  49.5 4.1 fusion.41
  53.7 5.2 reduce-scatter.13.cloned.1.call-done
  61.2 9.2 %reduce-scatter.11.cloned.1.call-done = f32[128,768]{1,0:T(8,128)} async-done(((f32[256,768]{1,0:T(8,128)}), f32[128,768]{1,0:T(8,128)}) %reduce-scatter.11.cloned.1.call-update) | async-done | bytes 393232 | tf_op jit(solution)/shard_map/reduce_scatter | solution.py:119
  70.4 2.9 fusion.44
  74.1 2.1 all_gather.15
  80.1 3.1 bitcast_reduce_fusion
  91.4 3.4 convolution_bitcast_fusion
  99.9 2.5 fusion.9
  103.4 4.5 fusion.40
  109.0 4.1 fusion.29
  113.9 77.1 %all-reduce.1 = (f32[2,384]{1,0:T(2,128)}, f32[1536]{0:T(1024)}) all-reduce(f32[2,384]{1,0:T(2,128)S(1)} %pad_maximum_fusion, f32[1536]{0:T(1024)S(1)} %copy-done.35), channel_id=1, replica_groups=mesh['dp'=16,'tensor'=2] {'dp'}, use_global_device_ids=true, to_apply=%region_21.22 | all-reduce | flops 2304 | bytes 18432 | tf_op jit(solution)/shard_map/psum | solution.py:182
  192.2 37.8 %all-reduce = (f32[768]{0:T(1024)}, f32[768]{0:T(1024)}, f32[768]{0:T(1024)}, f32[768]{0:T(1024)}, f32[768]{0:T(1024)}, /*index=5*/f32[768]{0:T(1024)}) all-reduce(f32[768]{0:T(1024)S(1)} %get-tuple-element.16, f32[768]{0:T(1024)S(1)} %get-tuple-element.21, ...), channel_id=1, replica_groups=mesh['dp'=16,'tensor'=2] {'dp','tensor'}, use_global_device_ids=true, to_apply=%region_15.16 | all-reduce | flops 4608 | bytes 36864 | tf_op jit(solution)/shard_map/psum | solution.py:171
  231.9 3.8 reduce-scatter.19.cloned.1.call-done
  235.7 139.6 %reduce-scatter.17.cloned.1.call-done = f32[48,3,384]{2,0,1:T(8,128)} async-done(((f32[768,3,384]{2,0,1:T(8,128)}), f32[48,3,384]{2,0,1:T(8,128)}) %reduce-scatter.17.cloned.1.call-update) | async-done | bytes 221200 | tf_op jit(solution)/shard_map/reduce_scatter | solution.py:166
  375.3 143.1 %reduce-scatter.23.cloned.1.call-done = f32[1536,48]{0,1:T(8,128)} async-done(((f32[1536,768]{0,1:T(8,128)}), f32[1536,48]{0,1:T(8,128)}) %reduce-scatter.23.cloned.1.call-update) | async-done | bytes 294928 | tf_op jit(solution)/shard_map/reduce_scatter | solution.py:169
  518.4 143.2 %reduce-scatter.21.cloned.1.call-done = f32[48,1536]{1,0:T(8,128)} async-done(((f32[768,1536]{1,0:T(8,128)}), f32[48,1536]{1,0:T(8,128)}) %reduce-scatter.21.cloned.1.call-update) | async-done | bytes 294928 | tf_op jit(solution)/shard_map/reduce_scatter | solution.py:168
  (150 shorter events, 44.3 us)
Async XLA Ops:
  7.2 36.2 %copy-start = (bf16[768,1536]{1,0:T(8,128)(2,1)S(1)}, bf16[768,1536]{1,0:T(8,128)(2,1)}, u32[]{:S(2)}) copy-start(bf16[768,1536]{1,0:T(8,128)(2,1)} %param.25) | copy-start | bytes 7077892
  7.2 31.7 %reduce-scatter.9.cloned.1.call-start = ((), (), s32[]{:S(2)}) async-start(), calls=%async_computation.8 | async-start | bytes 1179648 | tf_op jit(solution)/shard_map/reduce_scatter | solution.py:109
  20.5 5.0 copy-start.26
  28.0 30.9 %reduce-scatter.13.cloned.1.call-start = ((), (), s32[]{:S(2)}) async-start(), calls=%async_computation.10 | async-start | bytes 1179648 | tf_op jit(solution)/shard_map/reduce_scatter | solution.py:131
  30.9 8.0 %copy-start.3 = (bf16[128,768]{1,0:T(8,128)(2,1)S(1)}, bf16[128,768]{1,0:T(8,128)(2,1)}, u32[]{:S(2)}) copy-start(bf16[128,768]{1,0:T(8,128)(2,1)} %param.15) | copy-start | bytes 589828
  30.9 9.5 %copy-start.24 = (f32[768]{0:T(1024)S(1)}, f32[768]{0:T(1024)}, u32[]{:S(2)}) copy-start(f32[768]{0:T(1024)} %param.23) | copy-start | bytes 9220
  38.9 4.5 copy-start.16
  38.9 4.5 copy-start.42
  49.5 21.0 %reduce-scatter.11.cloned.1.call-start = ((), (), s32[]{:S(2)}) async-start(), calls=%async_computation.9 | async-start | bytes 1179648 | tf_op jit(solution)/shard_map/reduce_scatter | solution.py:119
  53.6 137.3 %reduce-scatter.15.cloned.1.call-start = ((), (), s32[]{:S(2)}) async-start(), calls=%async_computation.11 | async-start | bytes 1179648 | tf_op jit(solution)/shard_map/reduce_scatter | solution.py:161
  70.4 5.7 copy-start.11
  77.2 6.0 copy-start.27
  94.9 140.9 %reduce-scatter.19.cloned.1.call-start = ((), (), s32[]{:S(2)}) async-start(), calls=%async_computation.13 | async-start | bytes 1253376 | tf_op jit(solution)/shard_map/reduce_scatter | solution.py:167
  96.4 278.9 %reduce-scatter.17.cloned.1.call-start = ((), (), s32[]{:S(2)}) async-start(), calls=%async_computation.12 | async-start | bytes 3760128 | tf_op jit(solution)/shard_map/reduce_scatter | solution.py:166
  102.5 415.9 %reduce-scatter.23.cloned.1.call-start = ((), (), s32[]{:S(2)}) async-start(), calls=%async_computation.15 | async-start | bytes 5013504 | tf_op jit(solution)/shard_map/reduce_scatter | solution.py:169
  108.0 553.5 %reduce-scatter.21.cloned.1.call-start = ((), (), s32[]{:S(2)}) async-start(), calls=%async_computation.14 | async-start | bytes 5013504 | tf_op jit(solution)/shard_map/reduce_scatter | solution.py:168
  113.1 77.9 %copy-start.25 = (f32[768]{0:T(1024)S(1)}, f32[768]{0:T(1024)}, u32[]{:S(2)}) copy-start(f32[768]{0:T(1024)} %param.17) | copy-start | bytes 9220
  113.1 77.9 %copy-start.33 = (f32[128]{0:T(128)S(1)}, f32[128]{0:T(128)}, u32[]{:S(2)}) copy-start(f32[128]{0:T(128)} %copy-done.32) | copy-start | bytes 1540
  113.1 77.8 %copy-start.37 = (f32[128]{0:T(128)S(1)}, f32[128]{0:T(128)}, u32[]{:S(2)}) copy-start(f32[128]{0:T(128)} %copy-done.36) | copy-start | bytes 1540
  113.1 79.1 %copy-start.28 = (f32[768]{0:T(1024)S(1)}, f32[768]{0:T(1024)}, u32[]{:S(2)}) copy-start(f32[768]{0:T(1024)} %get-tuple-element.14) | copy-start | bytes 9220
  113.1 79.1 %copy-start.29 = (f32[768]{0:T(1024)S(1)}, f32[768]{0:T(1024)}, u32[]{:S(2)}) copy-start(f32[768]{0:T(1024)} %get-tuple-element.20) | copy-start | bytes 9220
  113.1 79.1 %copy-start.30 = (f32[768]{0:T(1024)S(1)}, f32[768]{0:T(1024)}, u32[]{:S(2)}) copy-start(f32[768]{0:T(1024)} %get-tuple-element.34) | copy-start | bytes 9220
  113.1 79.1 %copy-start.31 = (f32[768]{0:T(1024)S(1)}, f32[768]{0:T(1024)}, u32[]{:S(2)}) copy-start(f32[768]{0:T(1024)} %get-tuple-element.41) | copy-start | bytes 9220
  113.1 116.9 %copy-start.5 = (f32[128,768]{1,0:T(8,128)S(1)}, f32[128,768]{1,0:T(8,128)}, u32[]{:S(2)}) copy-start(f32[128,768]{1,0:T(8,128)} %copy-done.4) | copy-start | bytes 1179652
  (27 other events, 47.7 us)
Sparse Core Ops, SparseCore 0:
  28.1 10.7 reduce-scatter.8
  49.6 9.2 reduce-scatter.12
  61.1 9.2 reduce-scatter.10
  95.0 9.2 reduce-scatter.14
  109.5 126.1 reduce-scatter.18
  241.2 134.0 reduce-scatter.16
  381.0 137.2 reduce-scatter.22
  524.1 137.3 reduce-scatter.20
where the time goes:
time: 669 us; the launch traced here: 668 us
  waiting for transfers between devices  448 us (67%)
  blocking collectives  123 us (18%)
  matrix products  41.2 us (6%)
  local copies, waits for them, and re-layouts  22 us (3%)
  other arithmetic  18.3 us (3%)
  between operations  14.6 us (2%)
    reduce_scatter x1, waiting for transfers between devices, shards(): lax.psum_scatter(expand_grad, 'dp', scatter_dimension=0, tiled=True)  143 us
    reduce_scatter x1, waiting for transfers between devices, shards(): lax.psum_scatter(contract_grad, 'dp', scatter_dimension=1, tiled=True)  143 us
    reduce_scatter x1, waiting for transfers between devices, shards(): lax.psum_scatter(joined_grad, 'dp', scatter_dimension=0, tiled=True)  140 us
    psum x1, blocking collectives, shards(): unit_sums = lax.psum((bias_grad, expand_bias_grad), 'dp')  77.1 us
    psum x1, blocking collectives, shards(): lax.psum((first_gain_grad, first_shift_grad, output_bias_grad, feed_gain_...  37.8 us
  transfers between devices with their start and end apart: 8, of which 7 were waited for; matrix products, arithmetic and copies ran while one was open for 4% of the time, Pallas kernels for 0%

commit v1 on v0

--- a/solution.py
+++ b/solution.py
@@ -168,7 +168,7 @@
         lax.psum_scatter(expand_grad, "dp", scatter_dimension=0, tiled=True),
         lax.psum_scatter(contract_grad, "dp", scatter_dimension=1, tiled=True),
     )
-    row_sums = lax.psum(
+    partial = lax.psum(
         (
             first_gain_grad,
             first_shift_grad,
@@ -177,8 +177,9 @@
             feed_shift_grad,
             contract_bias_grad,
         ),
-        ("dp", "tensor"),
-    )
+        "tensor",
+    )
+    row_sums = lax.psum(partial, "dp")
     unit_sums = lax.psum((bias_grad, expand_bias_grad), "dp")
     return (
         block_output,

time: 669 us -> 668 us (level)
  waiting for transfers between devices: 448 us -> 482 us
  blocking collectives: 123 us -> 89.7 us
    psum x1, blocking collectives: 37.8 us -> 3.44 us  [shards(): lax.psum((first_gain_grad, first_shift_grad, output_bias_grad, feed_gain_...]
    reduce_scatter x1, waiting for transfers between devices: 3.77 us -> 37.3 us  [shards(): lax.psum_scatter(output_grad, 'dp', scatter_dimension=1, tiled=True)]
where the time goes in v1:
time: 668 us; the launch traced here: 667 us
  waiting for transfers between devices  482 us (72%)
  blocking collectives  89.7 us (13%)
  matrix products  41.3 us (6%)
  local copies, waits for them, and re-layouts  20.8 us (3%)
  other arithmetic  18.3 us (3%)
  between operations  14.7 us (2%)
    reduce_scatter x1, waiting for transfers between devices, shards(): lax.psum_scatter(expand_grad, 'dp', scatter_dimension=0, tiled=True)  143 us
    reduce_scatter x1, waiting for transfers between devices, shards(): lax.psum_scatter(contract_grad, 'dp', scatter_dimension=1, tiled=True)  143 us
    reduce_scatter x1, waiting for transfers between devices, shards(): lax.psum_scatter(joined_grad, 'dp', scatter_dimension=0, tiled=True)  139 us
    psum x1, blocking collectives, shards(): row_sums = lax.psum(partial, 'dp')  77.8 us
    reduce_scatter x1, waiting for transfers between devices, shards(): lax.psum_scatter(output_grad, 'dp', scatter_dimension=1, tiled=True)  37.3 us
  transfers between devices with their start and end apart: 8, of which 7 were waited for; matrix products, arithmetic and copies ran while one was open for 4% of the time, Pallas kernels for 0%

profile of v1, /device:TPU:0, one launch (start us, length us, event | category | flops | bytes accessed | tf_op | source)
XLA Modules:
  0.0 667.0 jit_solution(15860452528496530177)
XLA Ops:
  10.7 2.2 all_gather.12
  12.9 3.9 copy.44
  16.8 2.2 fusion
  27.5 2.1 all_gather.14
  29.6 3.8 fusion.50
  33.4 5.0 reduce-scatter.9.cloned.1.call-done
  40.8 2.1 all_gather.13
  42.9 3.5 fusion.42
  49.0 4.1 fusion.41
  53.2 5.2 reduce-scatter.13.cloned.1.call-done
  60.8 9.2 %reduce-scatter.11.cloned.1.call-done = f32[128,768]{1,0:T(8,128)} async-done(((f32[256,768]{1,0:T(8,128)}), f32[128,768]{1,0:T(8,128)}) %reduce-scatter.11.cloned.1.call-update) | async-done | bytes 393232 | tf_op jit(solution)/shard_map/reduce_scatter | solution.py:119
  70.0 2.9 fusion.44
  73.6 2.1 all_gather.15
  79.7 3.1 bitcast_reduce_fusion
  91.0 3.4 convolution_bitcast_fusion
  99.5 2.5 fusion.9
  103.0 4.5 fusion.40
  108.5 4.1 fusion.29
  114.7 3.4 all-reduce.1
  118.2 77.8 %all-reduce = (f32[768]{0:T(1024)}, f32[768]{0:T(1024)}, f32[2,384]{1,0:T(2,128)}, f32[768]{0:T(1024)}, f32[768]{0:T(1024)}, /*index=5*/f32[768]{0:T(1024)}, f32[1536]{0:T(1024)}, f32[768]{0:T(1024)}) all-reduce(f32[768]{0:T(1024)S(1)} %get-tuple-element.32, ...), channel_id=1, replica_groups=mesh['dp'=16,'tensor'=2] {'dp'}, use_global_device_ids=true, to_apply=%region_16.17 | all-reduce | flops 6912 | bytes 55296 | tf_op jit(solution)/shard_map/psum | solution.py:182
  197.9 37.3 %reduce-scatter.19.cloned.1.call-done = f32[384,48]{0,1:T(8,128)} async-done(((f32[384,768]{0,1:T(8,128)}), f32[384,48]{0,1:T(8,128)}) %reduce-scatter.19.cloned.1.call-update) | async-done | bytes 73744 | tf_op jit(solution)/shard_map/reduce_scatter | solution.py:167
  235.2 139.0 %reduce-scatter.17.cloned.1.call-done = f32[48,3,384]{2,0,1:T(8,128)} async-done(((f32[768,3,384]{2,0,1:T(8,128)}), f32[48,3,384]{2,0,1:T(8,128)}) %reduce-scatter.17.cloned.1.call-update) | async-done | bytes 221200 | tf_op jit(solution)/shard_map/reduce_scatter | solution.py:166
  374.2 142.6 %reduce-scatter.23.cloned.1.call-done = f32[1536,48]{0,1:T(8,128)} async-done(((f32[1536,768]{0,1:T(8,128)}), f32[1536,48]{0,1:T(8,128)}) %reduce-scatter.23.cloned.1.call-update) | async-done | bytes 294928 | tf_op jit(solution)/shard_map/reduce_scatter | solution.py:169
  516.9 143.3 %reduce-scatter.21.cloned.1.call-done = f32[48,1536]{1,0:T(8,128)} async-done(((f32[768,1536]{1,0:T(8,128)}), f32[48,1536]{1,0:T(8,128)}) %reduce-scatter.21.cloned.1.call-update) | async-done | bytes 294928 | tf_op jit(solution)/shard_map/reduce_scatter | solution.py:168
  (150 shorter events, 43.1 us)
Async XLA Ops:
  7.2 35.7 %copy-start = (bf16[768,1536]{1,0:T(8,128)(2,1)S(1)}, bf16[768,1536]{1,0:T(8,128)(2,1)}, u32[]{:S(2)}) copy-start(bf16[768,1536]{1,0:T(8,128)(2,1)} %param.25) | copy-start | bytes 7077892
  7.2 31.2 %reduce-scatter.9.cloned.1.call-start = ((), (), s32[]{:S(2)}) async-start(), calls=%async_computation.8 | async-start | bytes 1179648 | tf_op jit(solution)/shard_map/reduce_scatter | solution.py:109
  20.0 5.0 copy-start.26
  27.5 30.9 %reduce-scatter.13.cloned.1.call-start = ((), (), s32[]{:S(2)}) async-start(), calls=%async_computation.10 | async-start | bytes 1179648 | tf_op jit(solution)/shard_map/reduce_scatter | solution.py:131
  29.6 3.8 copy-start.8
  29.6 8.8 %copy-start.3 = (bf16[128,768]{1,0:T(8,128)(2,1)S(1)}, bf16[128,768]{1,0:T(8,128)(2,1)}, u32[]{:S(2)}) copy-start(bf16[128,768]{1,0:T(8,128)(2,1)} %param.15) | copy-start | bytes 589828
  29.6 10.3 %copy-start.24 = (f32[768]{0:T(1024)S(1)}, f32[768]{0:T(1024)}, u32[]{:S(2)}) copy-start(f32[768]{0:T(1024)} %param.23) | copy-start | bytes 9220
  38.4 4.5 copy-start.16
  38.4 4.5 copy-start.42
  42.9 3.5 copy-start.12
  49.0 21.0 %reduce-scatter.11.cloned.1.call-start = ((), (), s32[]{:S(2)}) async-start(), calls=%async_computation.9 | async-start | bytes 1179648 | tf_op jit(solution)/shard_map/reduce_scatter | solution.py:119
  53.1 60.3 %reduce-scatter.15.cloned.1.call-start = ((), (), s32[]{:S(2)}) async-start(), calls=%async_computation.11 | async-start | bytes 1179648 | tf_op jit(solution)/shard_map/reduce_scatter | solution.py:161
  70.0 5.7 copy-start.11
  76.8 6.0 copy-start.27
  78.5 4.2 copy-start.2
  78.5 4.2 copy-start.18
  78.5 4.2 copy-start.21
  78.5 4.2 copy-start.23
  94.4 140.8 %reduce-scatter.19.cloned.1.call-start = ((), (), s32[]{:S(2)}) async-start(), calls=%async_computation.13 | async-start | bytes 1253376 | tf_op jit(solution)/shard_map/reduce_scatter | solution.py:167
  95.9 278.3 %reduce-scatter.17.cloned.1.call-start = ((), (), s32[]{:S(2)}) async-start(), calls=%async_computation.12 | async-start | bytes 3760128 | tf_op jit(solution)/shard_map/reduce_scatter | solution.py:166
  102.0 414.9 %reduce-scatter.23.cloned.1.call-start = ((), (), s32[]{:S(2)}) async-start(), calls=%async_computation.15 | async-start | bytes 5013504 | tf_op jit(solution)/shard_map/reduce_scatter | solution.py:169
  107.6 552.6 %reduce-scatter.21.cloned.1.call-start = ((), (), s32[]{:S(2)}) async-start(), calls=%async_computation.14 | async-start | bytes 5013504 | tf_op jit(solution)/shard_map/reduce_scatter | solution.py:168
  112.7 5.5 copy-start.35
  112.7 83.3 %copy-start.5 = (f32[128,768]{1,0:T(8,128)S(1)}, f32[128,768]{1,0:T(8,128)}, u32[]{:S(2)}) copy-start(f32[128,768]{1,0:T(8,128)} %copy-done.4) | copy-start | bytes 1179652
  (27 other events, 37.1 us)
Sparse Core Ops, SparseCore 0:
  27.6 10.7 reduce-scatter.8
  49.1 9.2 reduce-scatter.12
  60.7 9.2 reduce-scatter.10
  94.5 9.2 reduce-scatter.14
  109.0 126.1 reduce-scatter.18
  240.7 133.4 reduce-scatter.16
  380.0 136.8 reduce-scatter.22
  522.6 137.5 reduce-scatter.20
